TPU v7x, 128 devices: a whole 4x4x4 slice. The times are simulated.
128 devices in a mesh: blk: 16 (over x, z_hi, core), kvh: 4 (over y), section: 2 (over z_lo).
Axes of the slice: x: 4, y: 4, z: 4 (z_hi: 2, z_lo: 2; z = z_hi * 2 + z_lo), core: 2. Of those that a mesh axis runs over, the one named last changes fastest.
Arguments:
- query: bfloat16 [8192, 3072], P('blk', ('kvh', 'section')), may hold values from -110 to 110
- keys: bfloat16 [8192, 1024], P('blk', ('kvh', 'section')), may hold values from -6 to 6
- values: bfloat16 [8192, 1024], P('blk', ('kvh', 'section')), may hold values from -6 to 6
- out_grad: bfloat16 [8192, 3072], P('blk', ('kvh', 'section')), may hold values from -96 to 96
- visible_from: int32 [8192], P('blk'), may hold values from 0 to 8191, as said below
- kv_input: bfloat16 [8192, 3072], P('blk', ('kvh', 'section')), may hold values from -60 to 60
- residual_grad: bfloat16 [8192, 3072], P('blk', ('kvh', 'section')), may hold values from -3 to 3
- ffn_input: bfloat16 [8192, 3072], P('blk', ('kvh', 'section')), may hold values from -60 to 60
- kv_gain: float32 [3072], replicated, may hold values from 0.25 to 1.75
- ffn_gain: float32 [3072], replicated, may hold values from 0.25 to 1.75
- w_key: bfloat16 [3072, 1024], P(('kvh', 'section')), may hold values from -0.109375 to 0.109375
- w_value: bfloat16 [3072, 1024], P(('kvh', 'section')), may hold values from -0.109375 to 0.109375
- w_gate: bfloat16 [3072, 4096], P(None, ('kvh', 'section')), may hold values from -0.109375 to 0.109375
- w_up: bfloat16 [3072, 4096], P(None, ('kvh', 'section')), may hold values from -0.109375 to 0.109375
- w_down: bfloat16 [4096, 3072], P(('kvh', 'section')), may hold values from -0.09375 to 0.09375
Outputs:
- query_grad: bfloat16 [8192, 3072], P('blk', ('kvh', 'section'))
- input_grad: bfloat16 [8192, 3072], P('blk', ('kvh', 'section'))
- key_weight_grad: bfloat16 [16, 3072, 1024], P('blk', ('kvh', 'section'))
- value_weight_grad: bfloat16 [16, 3072, 1024], P('blk', ('kvh', 'section'))
- gate_grad: bfloat16 [16, 3072, 4096], P('blk', None, ('kvh', 'section'))
- up_grad: bfloat16 [16, 3072, 4096], P('blk', None, ('kvh', 'section'))
- down_grad: bfloat16 [16, 4096, 3072], P('blk', ('kvh', 'section'))
Inputs may be any that keep to these rules, and one draw needn't show every extreme that they name: visible_from[t] is the first position of the document that holds position t: it is 0 at t = 0, never above t and never falling along t; the last position begins a document of its own.
All inputs are finite; a program needn't handle non-finite values.
Results may differ from a plain program's by a relative error of at most 0.02.
Values may be sent and summed in bfloat16 or wider, within the bound.
A program may use at most 192 MiB of HBM per device.

v0:
```python
import math

import jax
import jax.numpy as jnp
from jax import lax
from jax.sharding import Mesh
from jax.sharding import PartitionSpec as P

HEAD = 128
BLK = ("blk_0", "blk_1", "blk_2")


epsilon = 1e-06
lowest = -1e30


def reduced_to_own(blocks, axes, sequence):
    lengths = [lax.axis_size(a) for a in axes]
    blocks = blocks.reshape(*lengths, *blocks.shape[1:])
    blocks = blocks.transpose(*sequence, *range(len(axes), blocks.ndim))
    blocks = blocks.reshape(-1, *blocks.shape[len(axes) :])
    for k in sequence:
        blocks = lax.psum_scatter(blocks, axes[k], scatter_dimension=0, tiled=True)
    return blocks[0]


def split_up(value, dim, count):
    before, after = (value.shape[:dim], value.shape[dim + 1 :])
    return jnp.moveaxis(value.reshape(*before, count, -1, *after), dim, 0)


def scatter_axes(value, axes, sequence, dim):
    count = lax.axis_size(axes)
    return reduced_to_own(split_up(value, dim, count), axes, sequence)


def sent_to_all(value, axis):
    copies = jnp.broadcast_to(value, (lax.axis_size(axis), *value.shape))
    return lax.all_to_all(copies, axis, split_axis=0, concat_axis=0, tiled=True)


def in_order(blocks, dim):
    blocks = jnp.moveaxis(blocks, 0, dim)
    lengths = blocks.shape
    return blocks.reshape(*lengths[:dim], lengths[dim] * lengths[dim + 1], *lengths[dim + 2 :])


def gather_directly(value, axis, dim):
    blocks = sent_to_all(value, axis)
    return in_order(blocks, dim)


def side_by_side(arrays, axis, dim, along):
    ends, at = ([], 0)
    for a in arrays[:-1]:
        at += a.shape[along]
        ends.append(at)
    both = jnp.concatenate(arrays, axis=along)
    return tuple(jnp.split(lax.all_gather(both, axis, axis=dim, tiled=True), ends, axis=along))


def summed_on_arrival(value, axis, dim):
    blocks = split_up(value, dim, lax.axis_size(axis))
    arrived = lax.all_to_all(blocks, axis, split_axis=0, concat_axis=0, tiled=True)
    return arrived.astype(jnp.float32).sum(axis=0)


def over_copies(value, axis):
    return sent_to_all(value, axis).sum(axis=0)


def norm_rows(block):
    floats = block.astype(jnp.float32)
    inverse = lax.rsqrt(jnp.mean(floats * floats, axis=-1, keepdims=True) + epsilon)
    return (floats * inverse, inverse)


def contract_rows(left, right):
    return lax.dot_general(
        left, right, (((0,), (0,)), ((), ())), preferred_element_type=jnp.float32
    )


def contract_cols(left, right):
    return lax.dot_general(
        left, right, (((1,), (1,)), ((), ())), preferred_element_type=jnp.float32
    )


def on_device(
    query,
    keys,
    values,
    out_grad,
    visible_from,
    kv_input,
    residual_grad,
    ffn_input,
    kv_gain,
    ffn_gain,
    w_key,
    w_value,
    w_gate,
    w_up,
    w_down,
):
    rows = query.shape[0]
    width = keys.shape[1]
    local_heads = width // HEAD
    group = query.shape[1] // width
    scale = 1.0 / math.sqrt(HEAD)
    blocks = lax.axis_size(BLK)
    own_block = lax.axis_index(BLK)
    query_heads = query.reshape(rows, local_heads, group, HEAD)
    grad_heads = out_grad.reshape(rows, local_heads, group, HEAD)
    query_pos = own_block * rows + jnp.arange(rows, dtype=jnp.int32)
    first_visible = jnp.min(visible_from)
    own_pair = jnp.stack((keys, values))

    def needed(source):
        return (source <= own_block) & ((source + 1) * rows > first_visible)

    def block_scores(pair, source):
        key_pos = source * rows + jnp.arange(rows, dtype=jnp.int32)
        visible = (key_pos[None, :] <= query_pos[:, None]) & (
            key_pos[None, :] >= visible_from[:, None]
        )
        raw = (
            jnp.einsum(
                "qgsd,kgd->gsqk",
                query_heads,
                pair[0].reshape(rows, local_heads, HEAD),
                preferred_element_type=jnp.float32,
            )
            * scale
        )
        return (jnp.where(visible[None, None], raw, lowest), visible[None, None])

    def value_products(pair):
        return jnp.einsum(
            "qgsd,kgd->gsqk",
            grad_heads,
            pair[1].reshape(rows, local_heads, HEAD),
            preferred_element_type=jnp.float32,
        )

    def add_stats(stats, pair, source):
        running, total, weighted = stats
        masked, visible = block_scores(pair, source)
        new_max = jnp.maximum(running, jnp.max(masked, axis=-1))
        shrink = jnp.exp(running - new_max)
        probs = jnp.where(visible, jnp.exp(masked - new_max[..., None]), 0.0)
        dprobs = value_products(pair)
        return (
            new_max,
            total * shrink + jnp.sum(probs, axis=-1),
            weighted * shrink + jnp.sum(probs * dprobs, axis=-1),
        )

    def maybe_stats(stats, pair, source):
        return lax.cond(
            needed(source), lambda inner: add_stats(inner, pair, source), lambda inner: inner, stats
        )

    def block_grads(pair, source, log_total, delta):
        masked, visible = block_scores(pair, source)
        probs = jnp.exp(masked - log_total[..., None])
        dscores = probs * (value_products(pair) - delta[..., None])
        probs_b = probs.astype(jnp.bfloat16)
        dscores_b = dscores.astype(jnp.bfloat16)
        key_heads = pair[0].reshape(rows, local_heads, HEAD)
        query_part = jnp.einsum(
            "gsqk,kgd->qgsd", dscores_b, key_heads, preferred_element_type=jnp.float32
        )
        key_part = jnp.einsum(
            "gsqk,qgsd->kgd", dscores_b, query_heads, preferred_element_type=jnp.float32
        )
        value_part = jnp.einsum(
            "gsqk,qgsd->kgd", probs_b, grad_heads, preferred_element_type=jnp.float32
        )
        return (
            query_part,
            jnp.stack((key_part.reshape(rows, width), value_part.reshape(rows, width))),
        )

    stat_shape = (local_heads, group, rows)
    start_stats = (
        jnp.full(stat_shape, lowest, jnp.float32),
        jnp.zeros(stat_shape, jnp.float32),
        jnp.zeros(stat_shape, jnp.float32),
    )
    start_query = jnp.zeros((rows, local_heads, group, HEAD), jnp.float32)
    every = lax.all_gather(own_pair, BLK, axis=1, tiled=True)

    def pick(source):
        return lax.dynamic_slice_in_dim(every, source * rows, rows, 1)

    stats = lax.fori_loop(
        0, blocks, lambda source, inner: maybe_stats(inner, pick(source), source), start_stats
    )
    log_total = stats[0] + jnp.log(stats[1])
    delta = stats[2] / stats[1]

    def grad_block(source, carry):

        def update(inner):
            query_part, key_parts = block_grads(pick(source), source, log_total, delta)
            current = lax.dynamic_slice_in_dim(inner[0], source * rows, rows, 1)
            return (
                lax.dynamic_update_slice_in_dim(inner[0], current + key_parts, source * rows, 1),
                inner[1] + query_part,
            )

        return lax.cond(needed(source), update, lambda inner: inner, carry)

    start_buffer = jnp.zeros((2, blocks * rows, width), jnp.float32)
    buffer, query_acc = lax.fori_loop(0, blocks, grad_block, (start_buffer, start_query))
    sums = scatter_axes(buffer.astype(jnp.bfloat16), BLK, (2, 0, 1), 1).astype(jnp.float32)
    query_grad = (query_acc * scale).reshape(rows, query.shape[1]).astype(jnp.bfloat16)
    key_value = jnp.stack((sums[0] * scale, sums[1])).astype(jnp.bfloat16)
    all_heads = gather_directly(key_value, ("kvh", "section"), 2)
    normed_grad = (
        contract_cols(all_heads[0], w_key) + contract_cols(all_heads[1], w_value)
    ).astype(jnp.bfloat16)
    ffn_full, kv_full, residual_full, normed_full = side_by_side(
        (ffn_input, kv_input, residual_grad, normed_grad), ("kvh", "section"), 1, 0
    )
    part_width = kv_input.shape[1]
    offset = lax.axis_index(("kvh", "section")) * part_width
    kv_hat, kv_inverse = norm_rows(kv_full)
    kv_normed = (
        lax.dynamic_slice_in_dim(kv_hat, offset, part_width, 1)
        * lax.dynamic_slice_in_dim(kv_gain, offset, part_width, 0)
    ).astype(jnp.bfloat16)
    key_weight_grad = contract_rows(kv_normed, all_heads[0]).astype(jnp.bfloat16)[None]
    value_weight_grad = contract_rows(kv_normed, all_heads[1]).astype(jnp.bfloat16)[None]
    kv_scaled = kv_gain * normed_full.astype(jnp.float32)
    y_grad = (
        residual_full.astype(jnp.float32)
        + kv_inverse * (kv_scaled - kv_hat * jnp.mean(kv_scaled * kv_hat, axis=-1, keepdims=True))
    ).astype(jnp.bfloat16)
    ffn_hat, ffn_inverse = norm_rows(ffn_full)
    act_in = (ffn_hat * ffn_gain).astype(jnp.bfloat16)
    gate = jnp.dot(act_in, w_gate, preferred_element_type=jnp.float32)
    upper = jnp.dot(act_in, w_up, preferred_element_type=jnp.float32)
    gate_sigmoid = jax.nn.sigmoid(gate)
    gate_silu = gate * gate_sigmoid
    hidden = (gate_silu * upper).astype(jnp.bfloat16)
    down_grad = contract_rows(hidden, y_grad).astype(jnp.bfloat16)[None]
    hidden_grad = contract_cols(y_grad, w_down)
    gate_act = (hidden_grad * upper * gate_sigmoid * (1.0 + gate * (1.0 - gate_sigmoid))).astype(
        jnp.bfloat16
    )
    up_act = (hidden_grad * gate_silu).astype(jnp.bfloat16)
    gate_grad = contract_rows(act_in, gate_act).astype(jnp.bfloat16)[None]
    up_grad = contract_rows(act_in, up_act).astype(jnp.bfloat16)[None]
    partial_value = contract_cols(gate_act, w_gate) + contract_cols(up_act, w_up)
    hat_slice = lax.dynamic_slice_in_dim(ffn_hat, offset, part_width, 1)
    y_slice = lax.dynamic_slice_in_dim(y_grad, offset, part_width, 1).astype(jnp.float32)
    act_slice = summed_on_arrival(partial_value.astype(jnp.bfloat16), ("kvh", "section"), 1)
    scaled_slice = lax.dynamic_slice_in_dim(ffn_gain, offset, part_width, 0) * act_slice
    row_part = jnp.sum(scaled_slice * hat_slice, axis=-1, keepdims=True)
    correction = over_copies(row_part, ("kvh", "section")) / ffn_full.shape[1]
    input_grad = (y_slice + ffn_inverse * (scaled_slice - hat_slice * correction)).astype(
        jnp.bfloat16
    )
    return (
        query_grad,
        input_grad,
        key_weight_grad,
        value_weight_grad,
        gate_grad,
        up_grad,
        down_grad,
    )


def solution(mesh):
    finer = Mesh(
        mesh.devices.reshape(4, 2, 2, mesh.shape["kvh"], mesh.shape["section"]),
        ("blk_0", "blk_1", "blk_2", "kvh", "section"),
    )
    placed = (
        P(BLK, ("kvh", "section")),
        P(BLK, ("kvh", "section")),
        P(BLK, ("kvh", "section")),
        P(BLK, ("kvh", "section")),
        P(BLK),
        P(BLK, ("kvh", "section")),
        P(BLK, ("kvh", "section")),
        P(BLK, ("kvh", "section")),
        P(),
        P(),
        P(("kvh", "section"), None),
        P(("kvh", "section"), None),
        P(None, ("kvh", "section")),
        P(None, ("kvh", "section")),
        P(("kvh", "section"), None),
    )
    return jax.shard_map(
        on_device,
        mesh=finer,
        in_specs=placed,
        out_specs=(
            P(BLK, ("kvh", "section")),
            P(BLK, ("kvh", "section")),
            P(BLK, ("kvh", "section"), None),
            P(BLK, ("kvh", "section"), None),
            P(BLK, None, ("kvh", "section")),
            P(BLK, None, ("kvh", "section")),
            P(BLK, ("kvh", "section"), None),
        ),
        check_vma=False,
    )
```

profile of v0, /device:TPU:0, one launch (start us, length us, event | category | flops | bytes accessed | tf_op | source)
XLA Modules:
  0.0 667.9 jit_solution(4597913641544280654)
XLA Ops:
  7.2 1.8 pad_maximum_fusion.1
  9.2 1.9 copy.60
  11.1 1.2 copy.64
  12.3 1.9 copy.61
  14.2 1.9 copy.63
  16.1 0.6 reduce_min.9
  16.8 53.0 %all-gather.3.cloned.1.call-done = bf16[2,8192,128]{2,1,0:T(8,128)(2,1)} async-done(((bf16[2,512,128]{2,1,0:T(8,128)(2,1)}), bf16[2,8192,128]{2,1,0:T(8,128)(2,1)}) %all-gather.3.cloned.1.call-update) | async-done | bytes 4194320 | tf_op jit(solution)/shard_map/all_gather | solution.py:193
  70.4 26.8 %while.34 = (s32[]{:T(128)}, f32[1,3,512]{2,1,0:T(4,128)S(1)}, f32[1,3,512]{2,1,0:T(4,128)}, f32[1,3,512]{2,1,0:T(4,128)S(1)}, s32[]{:T(128)}, /*index=5*/s32[]{...) while((s32[]{:T(128)}, f32[1,3,512]{2,1,0:T(4,128)S(1)}, ...), condition=%wide.region_7.8_spmd.clone, body=%wide.region_1.7_spmd.clone.sunk | while | flops 414455296 | bytes 13281749 | solution.py:198
  71.6 7.0 %conditional.6 = ((f32[1,3,512]{2,1,0:T(4,128)S(1)}, f32[1,3,512]{2,1,0:T(4,128)}, f32[1,3,512]{2,1,0:T(4,128)S(1)})) conditional(s32[]{:T(128)} %convert_element_type.184, (f32[1,3,512]{2,1,0:T(4,128)S(1)}, f32[1,3,512]{2,1,0:T(4,128)}, f32[1,3,512]{2,1,0:T(4,128)S(1)}) %tuple.113, (s32[]{:T(128)}, s32[]{:T(128)}, s32[512]{0:T(512)}, ...), branch_computations={%region_2.0_spmd, %region_3.6_spmd} | conditional | flops 414455296 | bytes 13279426 | solution.py:161
  71.6 0.7 iota_add_fusion
  72.3 0.9 compare_and_fusion
  73.3 1.6 fusion.5
  74.9 2.2 fusion.4
  77.1 0.8 fusion.6
  97.1 1.3 fusion.65
  98.4 1.0 broadcast_in_dim.85
  99.4 3.8 broadcast_in_dim.84
  103.2 20.3 %while.35 = (s32[]{:T(128)}, f32[2,8192,128]{2,1,0:T(8,128)}, f32[512,1,3,128]{0,3,2,1:T(8,128)}, s32[]{:T(128)}, s32[]{:T(128)}, /*index=5*/s32[512]{0:T(512)S(...) while((s32[]{:T(128)}, f32[2,8192,128]{2,1,0:T(8,128)}, ...), condition=%wide.region_11.12_spmd.clone, body=%wide.region_8.11_spmd.clone.sunk | while | flops 1015743488 | bytes 28500472 | solution.py:217
  103.9 9.1 %conditional.7 = ((f32[2,8192,128]{2,1,0:T(8,128)}, f32[512,1,3,128]{0,3,2,1:T(8,128)})) conditional(s32[]{:T(128)} %convert_element_type.185, (f32[2,8192,128]{2,1,0:T(8,128)}, f32[512,1,3,128]{0,3,2,1:T(8,128)}) %tuple.116, (s32[]{:T(128)}, f32[2,8192,128]{2,1,0:T(8,128)}, s32[]{:T(128)}, s32[512]{0:T(512)S(1)}, bf16[2,8192,128]{2,1,0:T(8,128)(2,1)}, ...), branch_computations={%region_9.9_spmd, %region_10.10_spmd} | conditional | flops 1015743488 | bytes 28498142 | solution.py:214
  104.2 1.5 fusion.41
  105.7 0.9 fusion.31
  106.7 2.1 fusion.13
  108.8 1.3 fusion.28
  111.1 1.9 fusion.37
  123.6 3.9 convert_element_type.94
  127.5 2.2 copy.67
  129.8 93.4 %reduce-scatter.4.cloned.1.call-done = bf16[8,2,512,128]{3,2,1,0:T(8,128)(2,1)} async-done(((bf16[16,2,512,128]{3,2,1,0:T(8,128)(2,1)}), bf16[8,2,512,128]{3,2,1,0:T(8,128)(2,1)}) %reduce-scatter.4.cloned.1.call-update) | async-done | bytes 2097168 | tf_op jit(solution)/shard_map/reduce_scatter | solution.py:23
  223.3 33.4 %reduce-scatter.6.cloned.1.call-done = bf16[2,2,512,128]{3,2,1,0:T(8,128)(2,1)} async-done(((bf16[8,2,512,128]{3,2,1,0:T(8,128)(2,1)}), bf16[2,2,512,128]{3,2,1,0:T(8,128)(2,1)}) %reduce-scatter.6.cloned.1.call-update) | async-done | bytes 524304 | tf_op jit(solution)/shard_map/reduce_scatter | solution.py:23
  256.8 20.7 %reduce-scatter.8.cloned.1.call-done = bf16[1,2,512,128]{3,2,1,0:T(8,128)(2,1)} async-done(((bf16[2,2,512,128]{3,2,1,0:T(8,128)(2,1)}), bf16[1,2,512,128]{3,2,1,0:T(8,128)(2,1)}) %reduce-scatter.8.cloned.1.call-update) | async-done | bytes 262160 | tf_op jit(solution)/shard_map/reduce_scatter | solution.py:23
  277.5 0.9 slice_bitcast_fusion
  278.4 0.9 fusion.58
  279.4 0.7 pad_maximum_fusion.2
  280.1 1.1 copy.68
  281.4 30.6 %all_to_all.15 = bf16[8,2,512,128]{2,3,1,0:T(8,128)(2,1)S(1)} all-to-all(bf16[8,2,512,128]{2,3,1,0:T(8,128)(2,1)S(1)} %broadcast_in_dim.87), channel_id=1, replica_groups=mesh['blk_0'=4,'blk_1'=2,'blk_2'=2,'kvh'=4,'section'=2] {'kvh','section'}, dimensions={0} | all-to-all | bytes 4194304 | tf_op jit(solution)/shard_map/all_to_all | solution.py:39
  312.5 0.9 copy-done.6
  313.4 0.7 fusion.66
  314.2 0.8 fusion.55
  315.0 1.3 pad_maximum_fusion
  316.3 245.8 %all-gather.5.cloned.1.call-done = bf16[2048,3072]{1,0:T(8,128)(2,1)} async-done(((bf16[2048,384]{1,0:T(8,128)(2,1)}), bf16[2048,3072]{1,0:T(8,128)(2,1)}) %all-gather.5.cloned.1.call-update) | async-done | bytes 12582928 | tf_op jit(solution)/shard_map/all_gather | solution.py:59
  562.2 2.6 fusion.48
  564.8 7.2 %multiply_reduce_fusion = (f32[512]{0:T(512)S(1)}, f32[512]{0:T(512)S(1)}, f32[512,3072]{1,0:T(8,128)}) fusion(f32[3072]{0:T(1024)S(1)} %copy-done.28, bf16[2048,3072]{1,0:T(8,128)(2,1)} %all-gather.5.cloned.1.call-done, f32[512]{0:T(512)S(1)} %add_rsqrt_fusion.1), kind=kLoop, calls=%fused_computation.67 | loop fusion | flops 14154752 | bytes 15747072 | tf_op jit(solution)/shard_map/reduce_sum | solution.py:240
  572.0 2.4 copy-done.1
  574.4 1.8 fusion.62
  576.3 1.8 fusion.63
  578.1 5.5 convert_multiply_fusion
  583.7 2.1 multiply_convert_fusion.2
  585.9 1.9 fusion.67
  587.8 1.9 add_convert_fusion
  589.7 2.0 copy.79
  591.7 7.1 %all-to-all-start.1 = ((bf16[8,512,384]{2,1,0:T(8,128)(2,1)}), bf16[8,512,384]{2,1,0:T(8,128)(2,1)}, u32[]{:S(2)}, u32[]{:S(2)}) async-start(bf16[8,512,384]{2,1,0:T(8,128)(2,1)} %bitcast.191), calls=%async_computation.4 | async-start | bytes 6291456 | tf_op jit(solution)/shard_map/all_to_all | solution.py:64
  598.9 1.2 multiply_convert_fusion.5
  600.1 0.9 copy.71
  601.0 3.1 fusion.54
  604.1 5.5 fusion.52
  609.6 5.6 fusion.51
  615.2 5.5 fusion.50
  620.7 23.3 %all-to-all-done.1 = bf16[8,512,384]{2,1,0:T(8,128)(2,1)} async-done(((bf16[8,512,384]{2,1,0:T(8,128)(2,1)}), bf16[8,512,384]{2,1,0:T(8,128)(2,1)}, u32[]{:S(2)}, u32[]{:S(2)}) %all-to-all-start.1) | async-done | bytes 3145760 | tf_op jit(solution)/shard_map/all_to_all | solution.py:64
  644.1 2.4 convert_reduce_fusion
  646.5 0.9 copy-done.7
  647.4 1.4 multiply_reduce_fusion.1
  649.3 3.3 all-to-all-start.2
  652.7 3.0 fusion.53
  655.7 3.1 all-to-all-done.2
  658.8 2.5 add_convert_fusion.2
  (156 shorter events, 13.8 us)
Async XLA Ops:
  7.2 564.8 %copy-start = (bf16[3072,512]{1,0:T(8,128)(2,1)S(1)}, bf16[3072,512]{1,0:T(8,128)(2,1)}, u32[]{:S(2)}) copy-start(bf16[3072,512]{1,0:T(8,128)(2,1)} %param.35) | copy-start | bytes 9437188
  7.2 9.0 %copy-start.26 = (s32[512]{0:T(512)S(1)}, s32[512]{0:T(512)}, u32[]{:S(2)}) copy-start(s32[512]{0:T(512)} %param.27) | copy-start | bytes 6148
  7.2 62.6 %all-gather.3.cloned.1.call-start = ((), (), s32[]{:S(2)}) async-start(), calls=%async_computation.6 | async-start | bytes 4456448 | tf_op jit(solution)/shard_map/all_gather | solution.py:193
  9.1 214.1 %reduce-scatter.4.cloned.1.call-start = ((), (), s32[]{:S(2)}) async-start(), calls=%async_computation.7 | async-start | bytes 6291456 | tf_op jit(solution)/shard_map/reduce_scatter | solution.py:23
  71.6 3.3 copy-start.24
  77.1 0.8 copy-start.19
  78.0 0.6 copy-start.20
  99.4 3.8 copy-start.27
  99.4 3.8 copy-start.29
  103.9 1.8 copy-start.25
  103.9 1.8 copy-start.30
  106.7 2.2 copy-start.2
  110.2 0.9 copy-start.3
  129.8 127.0 %reduce-scatter.6.cloned.1.call-start = ((), (), s32[]{:S(2)}) async-start(), calls=%async_computation.8 | async-start | bytes 2621440 | tf_op jit(solution)/shard_map/reduce_scatter | solution.py:23
  223.2 54.3 %reduce-scatter.8.cloned.1.call-start = ((), (), s32[]{:S(2)}) async-start(), calls=%async_computation.9 | async-start | bytes 786432 | tf_op jit(solution)/shard_map/reduce_scatter | solution.py:23
  256.7 305.4 %all-gather.5.cloned.1.call-start = ((), (), s32[]{:S(2)}) async-start(), calls=%async_computation.10 | async-start | bytes 14155776 | tf_op jit(solution)/shard_map/all_gather | solution.py:59
  312.2 1.2 copy-start.13
  312.2 2.0 copy-start.14
  312.4 1.0 copy-start.6
  312.5 1.7 copy-start.5
  312.5 2.5 copy-start.21
  312.5 2.5 copy-start.22
  312.5 2.5 copy-start.23
  316.3 248.4 %copy-start.28 = (f32[3072]{0:T(1024)S(1)}, f32[3072]{0:T(1024)}, u32[]{:S(2)}) copy-start(f32[3072]{0:T(1024)} %param.31) | copy-start | bytes 36868
  564.8 9.6 %copy-start.1 = (bf16[2048,3072]{1,0:T(8,128)(2,1)S(1)}, bf16[2048,3072]{1,0:T(8,128)(2,1)}, u32[]{:S(2)}) copy-start(bf16[2048,3072]{1,0:T(8,128)(2,1)} %all-gather.5.cloned.1.call-done) | copy-start | bytes 37748740
  564.8 9.6 %copy-start.31 = (f32[3072]{0:T(1024)S(1)}, f32[3072]{0:T(1024)}, u32[]{:S(2)}) copy-start(f32[3072]{0:T(1024)} %param.32) | copy-start | bytes 36868
  574.4 1.9 copy-start.8
  576.3 7.4 %copy-start.9 = (f32[512,512]{1,0:T(8,128)}, f32[512,512]{1,0:T(8,128)S(1)}, u32[]{:S(2)}) copy-start(f32[512,512]{1,0:T(8,128)S(1)} %fusion.62) | copy-start | bytes 3145732
  578.1 5.6 copy-start.11
  578.1 5.6 copy-start.33
  583.7 2.1 copy-start.4
  585.8 1.9 copy-start.15
  585.9 1.9 copy-start.17
  591.7 52.4 %all-to-all-start.1 = ((bf16[8,512,384]{2,1,0:T(8,128)(2,1)}), bf16[8,512,384]{2,1,0:T(8,128)(2,1)}, u32[]{:S(2)}, u32[]{:S(2)}) async-start(bf16[8,512,384]{2,1,0:T(8,128)(2,1)} %bitcast.191), calls=%async_computation.4 | async-start | bytes 6291456 | tf_op jit(solution)/shard_map/all_to_all | solution.py:64
  601.0 3.1 copy-start.10
  601.0 3.1 copy-start.12
  604.1 5.5 copy-start.18
  604.1 5.5 copy-start.32
  609.6 5.6 copy-start.16
  646.5 0.9 copy-start.7
  649.3 9.5 %all-to-all-start.2 = ((f32[8,512,1]{1,2,0:T(1,128)}), f32[8,512,1]{1,2,0:T(1,128)S(1)}, u32[]{:S(2)}, u32[]{:S(2)}) async-start(f32[8,512,1]{1,2,0:T(1,128)} %broadcast_in_dim.88), calls=%async_computation.5 | async-start | bytes 32768 | tf_op jit(solution)/shard_map/all_to_all | solution.py:39
Sparse Core Ops, SparseCore 0:
  11.0 58.6 all-gather.2
  129.9 93.2 reduce-scatter.3
  225.6 31.0 reduce-scatter.5
  258.9 18.5 reduce-scatter.7
  316.5 245.6 all-gather.4
where the time goes:
time: 670 us; the launch traced here: 668 us
  waiting for transfers between devices  473 us (71%)
  matrix products  44 us (7%)
  other arithmetic  38.2 us (6%)
  local copies, waits for them, and re-layouts  35.4 us (5%)
  blocking collectives  30.6 us (5%)
  loops' own time  22 us (3%)
  between operations  14.1 us (2%)
  starting transfers between devices  10.6 us (2%)
    all_gather x1, waiting for transfers between devices, side_by_side(): lax.all_gather(both, axis, axis=dim, tiled=True)  246 us
    reduce_scatter x3, waiting for transfers between devices, reduced_to_own(): blocks = lax.psum_scatter(blocks, axes[k], scatter_dimension=0, tiled=True)  148 us
    all_gather x1, waiting for transfers between devices, on_device(): every = lax.all_gather(own_pair, BLK, axis=1, tiled=True)  53 us
    all_to_all x1, blocking collectives, sent_to_all(): return lax.all_to_all(copies, axis, split_axis=0, concat_axis=0, tiled=True)  30.6 us
    all_to_all x1, waiting for transfers between devices, summed_on_arrival(): lax.all_to_all(blocks, axis, split_axis=0, concat_axis=0, tiled=True)  23.3 us
    dot_general x5, matrix products, contract_rows(): lax.dot_general(left, right, (((0,), (0,)), ((), ())), preferred_element_...  22.7 us
  transfers between devices with their start and end apart: 7, of which 7 were waited for; matrix products, arithmetic and copies ran while one was open for 5% of the time, Pallas kernels for 0%

commit v1 on v0

v1 whole, which is shorter than its diff:
```python
import functools
import math

import jax
import jax.numpy as jnp
from jax import lax
from jax.experimental import pallas as pl
from jax.experimental.pallas import tpu as pltpu
from jax.sharding import Mesh
from jax.sharding import PartitionSpec as P

HEAD = 128
BLK = ("bx", "bz", "bc")
FEAT = ("kvh", "section")
MESH = pl.DeviceIdType.MESH
LOG2E = 1.4426950408889634
VMEM = pltpu.VMEM
F32 = jnp.float32
BF16 = jnp.bfloat16

epsilon = 1e-06


def contract_rows(left, right):
    return lax.dot_general(left, right, (((0,), (0,)), ((), ())), preferred_element_type=F32)


def contract_cols(left, right):
    return lax.dot_general(left, right, (((1,), (1,)), ((), ())), preferred_element_type=F32)


def run_all(*plans):
    live = list(plans)
    while live:
        for plan in list(live):
            try:
                next(plan)
            except StopIteration:
                live.remove(plan)


def meet(peers):
    barrier = pltpu.get_barrier_semaphore()
    for peer in peers:
        pl.semaphore_signal(barrier, inc=1, device_id=peer, device_id_type=MESH)
    pl.semaphore_wait(barrier, len(peers))


class Wire:
    def __init__(self, send_sem, recv_sem):
        self.send_sem, self.recv_sem, self.sent = send_sem, recv_sem, []

    def send(self, i, src, dst, peer):
        copy = pltpu.make_async_remote_copy(
            src_ref=src,
            dst_ref=dst,
            send_sem=self.send_sem.at[i],
            recv_sem=self.recv_sem.at[i],
            device_id=peer,
            device_id_type=MESH,
        )
        copy.start()
        self.sent.append(copy)

    def got(self, i, dst, peer):
        pltpu.make_async_remote_copy(
            src_ref=dst,
            dst_ref=dst,
            send_sem=self.send_sem.at[i],
            recv_sem=self.recv_sem.at[i],
            device_id=peer,
            device_id_type=MESH,
        ).wait_recv()

    def finish(self):
        for copy in self.sent:
            copy.wait_send()


def feat_place():
    y, z = lax.axis_index("kvh"), lax.axis_index("section")
    return y, lax.rem(y + 1, 4), lax.rem(y + 3, 4), lax.rem(y + 2, 4), z, 1 - z


def feat_peers():
    y, yp, ym, y2, z, zo = feat_place()
    return [{"kvh": yp}, {"kvh": ym}, {"section": zo}]


def feat_others():
    y, yp, ym, y2, z, zo = feat_place()
    others = [{"section": zo}]
    for other in (yp, ym, y2):
        others.append({"kvh": other})
        others.append({"kvh": other, "section": zo})
    return others


def blk_place():
    x, z, c = lax.axis_index("bx"), lax.axis_index("bz"), lax.axis_index("bc")
    return x, lax.rem(x + 1, 4), lax.rem(x + 3, 4), lax.rem(x + 2, 4), z, 1 - z, c, 1 - c


def blk_peers():
    x, xp, xm, x2, z, zo, c, co = blk_place()
    return [{"bx": xp}, {"bx": xm}, {"bz": zo}, {"bc": co}]


GATHER8 = 18


def gather8(wire, x_ref, out_ref, cut):
    y, yp, ym, y2, z, zo = feat_place()
    rows, cols = x_ref.shape
    p_y, m_y, o_z = {"kvh": yp}, {"kvh": ym}, {"section": zo}
    full_a, low_a, high_a = (0, cut), (0, cut // 2), (cut // 2, cut // 2)
    rest = rows - cut
    full_b, low_b, high_b = (cut, rest), (cut, rest // 2), (cut + rest // 2, rest // 2)

    def at(sy, sz, part):
        start = pl.multiple_of((sy * 2 + sz) * cols, cols)
        return out_ref.at[pl.ds(part[0], part[1]), pl.ds(start, cols)]

    def own(i, part, peer):
        wire.send(i, x_ref.at[pl.ds(part[0], part[1]), :], at(y, z, part), peer)

    def on(i, sy, sz, part, peer):
        wire.send(i, at(sy, sz, part), at(sy, sz, part), peer)

    def got(i, sy, sz, part):
        wire.got(i, at(sy, sz, part), o_z)

    own(0, full_a, o_z)
    own(1, full_a, p_y)
    own(2, full_a, m_y)
    own(3, full_b, p_y)
    own(4, full_b, m_y)
    own(5, full_b, o_z)
    yield
    got(0, y, zo, full_a)
    on(6, y, zo, full_a, p_y)
    on(7, y, zo, full_a, m_y)
    yield
    got(1, ym, z, full_a)
    on(8, ym, z, low_a, p_y)
    yield
    got(2, yp, z, full_a)
    on(9, yp, z, high_a, m_y)
    yield
    got(3, ym, z, full_b)
    on(10, ym, z, low_b, p_y)
    on(12, ym, z, full_b, o_z)
    yield
    got(4, yp, z, full_b)
    on(11, yp, z, high_b, m_y)
    on(13, yp, z, full_b, o_z)
    yield
    got(6, ym, zo, full_a)
    on(14, ym, zo, low_a, p_y)
    yield
    got(7, yp, zo, full_a)
    on(15, yp, zo, high_a, m_y)
    yield
    got(10, y2, z, low_b)
    on(16, y2, z, low_b, o_z)
    yield
    got(11, y2, z, high_b)
    on(17, y2, z, high_b, o_z)
    yield
    got(5, y, zo, full_b)
    got(8, y2, z, low_a)
    got(9, y2, z, high_a)
    got(12, ym, zo, full_b)
    got(13, yp, zo, full_b)
    got(14, y2, zo, low_a)
    got(15, y2, zo, high_a)
    got(16, y2, zo, low_b)
    got(17, y2, zo, high_b)
    wire.finish()


GATHER16 = 19


def gather16(wire, kv_ref, out_ref):
    x, xp, xm, x2, z, zo, c, co = blk_place()
    rows = kv_ref.shape[1]
    p_x, m_x, o_z, o_c = {"bx": xp}, {"bx": xm}, {"bz": zo}, {"bc": co}
    full, low, high = (0, rows), (0, rows // 2), (rows // 2, rows // 2)

    def at(sx, sz, sc, part):
        return out_ref.at[:, sx * 4 + sz * 2 + sc, pl.ds(part[0], part[1]), :]

    def own(i, peer):
        wire.send(i, kv_ref, at(x, z, c, full), peer)

    def on(i, sx, sz, part, peer):
        wire.send(i, at(sx, sz, c, part), at(sx, sz, c, part), peer)

    def got(i, sx, sz, part, sc=None):
        wire.got(i, at(sx, sz, c if sc is None else sc, part), o_z)

    own(0, o_z)
    own(1, p_x)
    own(2, m_x)
    own(3, o_c)
    yield
    got(0, x, zo, full)
    on(4, x, zo, full, p_x)
    on(5, x, zo, full, m_x)
    on(6, x, zo, full, o_c)
    yield
    got(1, xm, z, full)
    on(7, xm, z, low, p_x)
    on(8, xm, z, full, o_c)
    yield
    got(2, xp, z, full)
    on(9, xp, z, high, m_x)
    on(10, xp, z, full, o_c)
    yield
    got(4, xm, zo, full)
    on(11, xm, zo, low, p_x)
    on(12, xm, zo, full, o_c)
    yield
    got(5, xp, zo, full)
    on(13, xp, zo, high, m_x)
    on(14, xp, zo, full, o_c)
    yield
    got(7, x2, z, low)
    on(15, x2, z, low, o_c)
    yield
    got(9, x2, z, high)
    on(16, x2, z, high, o_c)
    yield
    got(11, x2, zo, low)
    on(17, x2, zo, low, o_c)
    yield
    got(13, x2, zo, high)
    on(18, x2, zo, high, o_c)
    yield
    got(3, x, z, full, co)
    got(6, x, zo, full, co)
    got(8, xm, z, full, co)
    got(10, xp, z, full, co)
    got(12, xm, zo, full, co)
    got(14, xp, zo, full, co)
    got(15, x2, z, low, co)
    got(16, x2, z, high, co)
    got(17, x2, zo, low, co)
    got(18, x2, zo, high, co)
    wire.finish()


def first_kernel(kv_ref, ffn_ref, kv_out, ffn_out, s0, r0, s1, r1, local):
    x, xp, xm, x2, z, zo, c, co = blk_place()
    y, yp, ym, y2, sz, szo = feat_place()
    cols = ffn_ref.shape[1]
    meet(blk_peers() + feat_peers())
    keep_kv = pltpu.make_async_copy(kv_ref, kv_out.at[:, x * 4 + z * 2 + c], local.at[0])
    keep_ffn = pltpu.make_async_copy(
        ffn_ref,
        ffn_out.at[:, pl.ds(pl.multiple_of((y * 2 + sz) * cols, cols), cols)],
        local.at[1],
    )
    wire_kv, wire_ffn = Wire(s0, r0), Wire(s1, r1)
    kv_plan = gather16(wire_kv, kv_ref, kv_out)
    ffn_plan = gather8(wire_ffn, ffn_ref, ffn_out, ffn_ref.shape[0] * 3 // 4)
    next(kv_plan)
    next(ffn_plan)
    keep_kv.start()
    keep_ffn.start()
    run_all(kv_plan, ffn_plan)
    keep_kv.wait()
    keep_ffn.wait()


def gather_first(kv, ffn):
    rows, cols = ffn.shape
    return pl.pallas_call(
        first_kernel,
        name="gather_first",
        out_shape=(
            jax.ShapeDtypeStruct((2, 16, *kv.shape[1:]), kv.dtype),
            jax.ShapeDtypeStruct((rows, 8 * cols), ffn.dtype),
        ),
        in_specs=[pl.BlockSpec(memory_space=VMEM)] * 2,
        out_specs=(pl.BlockSpec(memory_space=pl.ANY),) * 2,
        scratch_shapes=[
            pltpu.SemaphoreType.DMA((GATHER16,)),
            pltpu.SemaphoreType.DMA((GATHER16,)),
            pltpu.SemaphoreType.DMA((GATHER8,)),
            pltpu.SemaphoreType.DMA((GATHER8,)),
            pltpu.SemaphoreType.DMA((2,)),
        ],
        compiler_params=pltpu.CompilerParams(collective_id=1, has_side_effects=True),
    )(kv, ffn)


def gather_kernel(x_ref, out_ref, s0, r0, local):
    y, yp, ym, y2, z, zo = feat_place()
    rows, cols = x_ref.shape
    meet(feat_peers())
    keep = pltpu.make_async_copy(
        x_ref,
        out_ref.at[:, pl.ds(pl.multiple_of((y * 2 + z) * cols, cols), cols)],
        local.at[0],
    )
    plan = gather8(Wire(s0, r0), x_ref, out_ref, rows // 2)
    next(plan)
    keep.start()
    run_all(plan)
    keep.wait()


def gather_features(x, collective_id):
    rows, cols = x.shape
    return pl.pallas_call(
        gather_kernel,
        name=f"gather_{collective_id}",
        out_shape=jax.ShapeDtypeStruct((rows, 8 * cols), x.dtype),
        in_specs=[pl.BlockSpec(memory_space=VMEM)],
        out_specs=pl.BlockSpec(memory_space=pl.ANY),
        scratch_shapes=[
            pltpu.SemaphoreType.DMA((GATHER8,)),
            pltpu.SemaphoreType.DMA((GATHER8,)),
            pltpu.SemaphoreType.DMA((1,)),
        ],
        compiler_params=pltpu.CompilerParams(collective_id=collective_id, has_side_effects=True),
    )(x)


def add(*terms):
    total = terms[0].astype(F32)
    for term in terms[1:]:
        total = total + term.astype(F32)
    return total


def ring_plan(wire, first, far, plus, minus, half, ring, near_p, near_m, far_p, far_m, p, m):
    low, high = half
    wire.send(first + 0, high(far), high(far_m), p)
    wire.send(first + 1, low(far), low(far_p), m)
    wire.send(first + 2, low(plus), low(near_m), p)
    wire.send(first + 3, high(minus), high(near_p), m)
    yield
    wire.got(first + 0, high(far_m), p)
    high(plus)[...] = add(high(plus)[...], high(far_m)[...]).astype(BF16)
    wire.send(first + 4, high(plus), high(near_m), p)
    yield
    wire.got(first + 1, low(far_p), p)
    low(minus)[...] = add(low(minus)[...], low(far_p)[...]).astype(BF16)
    wire.send(first + 5, low(minus), low(near_p), m)
    yield
    wire.got(first + 2, low(near_m), p)
    wire.got(first + 3, high(near_p), p)
    wire.got(first + 4, high(near_m), p)
    wire.got(first + 5, low(near_p), p)


SCATTER16 = 8 + 6 + 6 + 1


def scatter16_kernel(part_ref, out_ref, twin, acc, near, far, zsend, zrecv, ssem, rsem):
    x, xp, xm, x2, z, zo, c, co = blk_place()
    rows = part_ref.shape[2]
    half_rows = rows // 2
    wire = Wire(ssem, rsem)
    meet(blk_peers())
    order = [(tx, tz) for tz in (zo, z) for tx in (x2, xp, xm, x)]
    for i, (tx, tz) in enumerate(order):
        wire.send(i, part_ref.at[:, tx * 4 + tz * 2 + co], twin.at[i], {"bc": co})

    def merge(i):
        tx, tz = order[i]
        wire.got(i, twin.at[i], {"bc": co})
        acc[i] = add(part_ref[:, tx * 4 + tz * 2 + c], twin[i]).astype(BF16)

    def low(ref):
        return ref.at[:, pl.ds(0, half_rows), :]

    def high(ref):
        return ref.at[:, pl.ds(half_rows, half_rows), :]

    def ring(plane):
        base = plane * 4
        return ring_plan(
            wire,
            8 + plane * 6,
            acc.at[base],
            acc.at[base + 1],
            acc.at[base + 2],
            (low, high),
            None,
            near.at[plane, 0],
            near.at[plane, 1],
            far.at[plane, 0],
            far.at[plane, 1],
            {"bx": xp},
            {"bx": xm},
        )

    for i in range(3):
        merge(i)
    outer = ring(0)
    next(outer)
    for i in range(4, 7):
        merge(i)
    inner = ring(1)
    next(inner)
    merge(3)
    merge(7)
    run_all(outer)
    zsend[...] = add(acc[3], near[0, 0], near[0, 1]).astype(BF16)
    wire.send(20, zsend, zrecv, {"bz": zo})
    run_all(inner)
    total = add(acc[7], near[1, 0], near[1, 1])
    wire.got(20, zrecv, {"bz": zo})
    out_ref[...] = (total + zrecv[...].astype(F32)).astype(BF16)
    wire.finish()


def scatter_blocks(parts):
    _, _, rows, width = parts.shape
    shard = (2, rows, width)
    return pl.pallas_call(
        scatter16_kernel,
        name="scatter_blocks",
        out_shape=jax.ShapeDtypeStruct(shard, BF16),
        in_specs=[pl.BlockSpec(memory_space=VMEM)],
        out_specs=pl.BlockSpec(memory_space=VMEM),
        scratch_shapes=[
            VMEM((8, *shard), BF16),
            VMEM((8, *shard), BF16),
            VMEM((2, 2, *shard), BF16),
            VMEM((2, 2, *shard), BF16),
            VMEM(shard, BF16),
            VMEM(shard, BF16),
            pltpu.SemaphoreType.DMA((SCATTER16,)),
            pltpu.SemaphoreType.DMA((SCATTER16,)),
        ],
        compiler_params=pltpu.CompilerParams(collective_id=2, has_side_effects=True),
    )(parts)


def sum_stat_kernel(x_ref, out_ref, slots, ssem, rsem):
    others = feat_others()
    meet(others)
    wire = Wire(ssem, rsem)
    for i, peer in enumerate(others):
        wire.send(i, x_ref, slots.at[i], peer)
    total = x_ref[...]
    for i, peer in enumerate(others):
        wire.got(i, slots.at[i], peer)
        total = total + slots[i]
    out_ref[...] = total
    wire.finish()


def sum_stat(x, collective_id):
    return pl.pallas_call(
        sum_stat_kernel,
        name=f"sum_stat_{collective_id}",
        out_shape=jax.ShapeDtypeStruct(x.shape, F32),
        in_specs=[pl.BlockSpec(memory_space=VMEM)],
        out_specs=pl.BlockSpec(memory_space=VMEM),
        scratch_shapes=[
            VMEM((7, *x.shape), F32),
            pltpu.SemaphoreType.DMA((7,)),
            pltpu.SemaphoreType.DMA((7,)),
        ],
        compiler_params=pltpu.CompilerParams(collective_id=collective_id, has_side_effects=True),
    )(x)


SCATTER8 = 13 + 4 + 6


def scatter8_kernel(
    part_ref, stat_ref, out_ref, stat_out, acc, zbuf, near, far, zsend, zrecv, slots, ssem, rsem, s1, r1
):
    y, yp, ym, y2, z, zo = feat_place()
    rows, cols = out_ref.shape
    cut = rows // 2
    quarter = cut // 2
    others = feat_others()
    meet(others)
    wire, stat_wire = Wire(ssem, rsem), Wire(s1, r1)
    for i, peer in enumerate(others):
        stat_wire.send(i, stat_ref, slots.at[i], peer)

    def cols_of(ty, tz):
        return pl.ds(pl.multiple_of((ty * 2 + tz) * cols, cols), cols)

    def low(ref):
        return ref.at[pl.ds(0, quarter), :]

    def high(ref):
        return ref.at[pl.ds(quarter, quarter), :]

    def ring(plane, first):
        return ring_plan(
            wire,
            first,
            acc.at[plane, 0],
            acc.at[plane, 1],
            acc.at[plane, 2],
            (low, high),
            None,
            near.at[plane, 0],
            near.at[plane, 1],
            far.at[plane, 0],
            far.at[plane, 1],
            {"kvh": yp},
            {"kvh": ym},
        )

    turn = (y2, yp, ym, y)
    for i, ty in enumerate(turn):
        wire.send(i, part_ref.at[pl.ds(cut, cut), cols_of(ty, zo)], zbuf.at[i], {"section": zo})
    for i, ty in enumerate(turn):
        acc[0, i] = part_ref[pl.ds(0, cut), cols_of(ty, zo)]
    outer = ring(0, 4)
    next(outer)
    for i, ty in enumerate(turn):
        acc[1, i] = part_ref[pl.ds(0, cut), cols_of(ty, z)]
    inner = ring(1, 10)
    next(inner)
    for i, ty in enumerate(turn):
        wire.got(i, zbuf.at[i], {"section": zo})
        acc[2, i] = add(part_ref[pl.ds(cut, cut), cols_of(ty, z)], zbuf[i]).astype(BF16)
    last = ring(2, 16)
    next(last)
    run_all(outer)
    zsend[...] = add(acc[0, 3], near[0, 0], near[0, 1]).astype(BF16)
    wire.send(22, zsend, zrecv, {"section": zo})
    run_all(inner)
    total = add(acc[1, 3], near[1, 0], near[1, 1])
    run_all(last)
    out_ref[pl.ds(cut, cut), :] = add(acc[2, 3], near[2, 0], near[2, 1])
    stat = stat_ref[...]
    for i, peer in enumerate(others):
        stat_wire.got(i, slots.at[i], peer)
        stat = stat + slots[i]
    stat_out[...] = stat
    wire.got(22, zrecv, {"section": zo})
    out_ref[pl.ds(0, cut), :] = total + zrecv[...].astype(F32)
    wire.finish()
    stat_wire.finish()


def scatter_features(part, stat, collective_id):
    rows, width = part.shape
    cols = width // 8
    cut = rows // 2
    return pl.pallas_call(
        scatter8_kernel,
        name="scatter_features",
        out_shape=(
            jax.ShapeDtypeStruct((rows, cols), F32),
            jax.ShapeDtypeStruct(stat.shape, F32),
        ),
        in_specs=[pl.BlockSpec(memory_space=VMEM)] * 2,
        out_specs=(pl.BlockSpec(memory_space=VMEM),) * 2,
        scratch_shapes=[
            VMEM((3, 4, cut, cols), BF16),
            VMEM((4, cut, cols), BF16),
            VMEM((3, 2, cut, cols), BF16),
            VMEM((3, 2, cut, cols), BF16),
            VMEM((cut, cols), BF16),
            VMEM((cut, cols), BF16),
            VMEM((7, *stat.shape), F32),
            pltpu.SemaphoreType.DMA((SCATTER8,)),
            pltpu.SemaphoreType.DMA((SCATTER8,)),
            pltpu.SemaphoreType.DMA((7,)),
            pltpu.SemaphoreType.DMA((7,)),
        ],
        compiler_params=pltpu.CompilerParams(collective_id=collective_id, has_side_effects=True),
    )(part, stat)


MASKED = -1e30
START = -1e29


def attention_kernel(
    span_ref, seen_ref, q_ref, g_ref, kv_ref, dq_ref, dkv_ref,
    q_cat, g_cat, q_t, g_t, run_max, run_sum, run_dot, dq_t, *, tile, scale
):
    rows = q_ref.shape[0]
    group = q_ref.shape[1] // HEAD
    own, lowest, highest = span_ref[0], span_ref[1], span_ref[2]
    to_log2 = scale * LOG2E
    for h in range(group):
        for src, cat, turned in ((q_ref, q_cat, q_t), (g_ref, g_cat, g_t)):
            block = src[:, h * HEAD : (h + 1) * HEAD]
            cat[h * rows : (h + 1) * rows, :] = block
            turned[:, h * rows : (h + 1) * rows] = block.astype(F32).T.astype(BF16)
    run_max[...] = jnp.full_like(run_max, START)
    run_sum[...] = jnp.zeros_like(run_sum)
    run_dot[...] = jnp.zeros_like(run_dot)
    dq_t[...] = jnp.zeros_like(dq_t)

    tiles = dkv_ref.shape[1] // tile
    first = lowest // tile
    last = ((own + 1) * rows) // tile
    whole_from = jnp.minimum((highest + tile - 1) // tile, (own * rows) // tile)
    whole_to = (own * rows) // tile

    def part(j):
        return pl.ds(pl.multiple_of(j * tile, tile), tile)

    def lanes(h):
        return pl.ds(h * rows, rows)

    def scores(j, h, masked):
        keys = kv_ref[0, part(j), :]
        value = jnp.dot(keys, q_t[:, lanes(h)], preferred_element_type=F32) * to_log2
        if masked:
            key_pos = j * tile + lax.broadcasted_iota(jnp.int32, (tile, rows), 0)
            query_pos = own * rows + lax.broadcasted_iota(jnp.int32, (tile, rows), 1)
            visible = (key_pos <= query_pos) & (key_pos >= seen_ref[...])
            value = jnp.where(visible, value, MASKED)
        return value

    def products(j, h):
        return jnp.dot(kv_ref[1, part(j), :], g_t[:, lanes(h)], preferred_element_type=F32)

    def stats(j, masked):
        for h in range(group):
            value = scores(j, h, masked).reshape(tile // 8, 8, rows)
            dprobs = products(j, h).reshape(tile // 8, 8, rows)
            before = run_max[:, lanes(h)]
            now = jnp.maximum(before, jnp.max(value, axis=0))
            shrink = jnp.exp2(before - now)
            probs = jnp.exp2(value - now[None])
            run_max[:, lanes(h)] = now
            run_sum[:, lanes(h)] = run_sum[:, lanes(h)] * shrink + jnp.sum(probs, axis=0)
            run_dot[:, lanes(h)] = run_dot[:, lanes(h)] * shrink + jnp.sum(probs * dprobs, axis=0)

    def grads(j, masked):
        keys = kv_ref[0, part(j), :]
        value_part = jnp.zeros((tile, HEAD), F32)
        key_part = jnp.zeros((tile, HEAD), F32)
        for h in range(group):
            value = scores(j, h, masked)
            probs = jnp.exp2(value - run_max[0:1, lanes(h)])
            dscores = (probs * (products(j, h) - run_dot[0:1, lanes(h)])).astype(BF16)
            value_part = value_part + jnp.dot(
                probs.astype(BF16), g_cat[lanes(h), :], preferred_element_type=F32
            )
            key_part = key_part + jnp.dot(dscores, q_cat[lanes(h), :], preferred_element_type=F32)
            dq_t[:, lanes(h)] += contract_rows(keys, dscores)
        dkv_ref[0, part(j), :] = (key_part * scale).astype(BF16)
        dkv_ref[1, part(j), :] = value_part.astype(BF16)

    def sweep(body):
        lax.fori_loop(first, whole_from, lambda j, _: (body(j, True), 0)[1], 0)
        lax.fori_loop(jnp.maximum(whole_from, first), whole_to, lambda j, _: (body(j, False), 0)[1], 0)
        lax.fori_loop(jnp.maximum(whole_to, first), last, lambda j, _: (body(j, True), 0)[1], 0)

    sweep(stats)
    peak = jnp.max(run_max[...], axis=0, keepdims=True)
    factor = jnp.exp2(run_max[...] - peak)
    total = jnp.sum(run_sum[...] * factor, axis=0, keepdims=True)
    delta = jnp.sum(run_dot[...] * factor, axis=0, keepdims=True) / total
    run_max[0:1, :] = peak + jnp.log(total) * LOG2E
    run_dot[0:1, :] = delta

    def clear(j, _):
        dkv_ref[:, part(j), :] = jnp.zeros((2, tile, HEAD), BF16)
        return 0

    lax.fori_loop(0, first, clear, 0)
    lax.fori_loop(last, tiles, clear, 0)
    sweep(grads)
    for h in range(group):
        dq_ref[:, h * HEAD : (h + 1) * HEAD] = (dq_t[:, lanes(h)] * scale).T.astype(BF16)


def attention(query, out_grad, kv, visible_from, own, tile=256):
    rows, width = query.shape
    group = width // HEAD
    span = jnp.stack((own, visible_from[0], visible_from[-1])).astype(jnp.int32)
    cat = VMEM((group * rows, HEAD), BF16)
    turned = VMEM((HEAD, group * rows), BF16)
    stat = VMEM((8, group * rows), F32)
    return pl.pallas_call(
        functools.partial(attention_kernel, tile=tile, scale=1.0 / math.sqrt(HEAD)),
        name="attention",
        out_shape=(
            jax.ShapeDtypeStruct((rows, width), BF16),
            jax.ShapeDtypeStruct(kv.shape, BF16),
        ),
        in_specs=[pl.BlockSpec(memory_space=pltpu.SMEM)] + [pl.BlockSpec(memory_space=VMEM)] * 4,
        out_specs=(pl.BlockSpec(memory_space=VMEM),) * 2,
        scratch_shapes=[
            cat, cat, turned, turned, stat, stat, stat, VMEM((HEAD, group * rows), F32),
        ],
    )(span, visible_from.reshape(1, rows), query, out_grad, kv)


def inverse_of(squares, width):
    return lax.rsqrt(squares / width + epsilon)


def on_device(
    query, keys, values, out_grad, visible_from, kv_input, residual_grad, ffn_input,
    kv_gain, ffn_gain, w_key, w_value, w_gate, w_up, w_down,
):
    rows, part_width = query.shape
    width = kv_gain.shape[0]
    own = lax.axis_index(BLK)
    offset = lax.axis_index(FEAT) * part_width

    def mine(vector):
        return lax.dynamic_slice_in_dim(vector, offset, part_width, 0)

    every, ffn_full = gather_first(jnp.stack((keys, values)), ffn_input)
    blocks = every.shape[1]
    query_grad, dkv = attention(
        query, out_grad, every.reshape(2, blocks * rows, HEAD), visible_from, own
    )
    key_value = scatter_blocks(dkv.reshape(2, blocks, rows, HEAD))
    all_heads = gather_features(key_value.reshape(2 * rows, HEAD), 3)
    key_heads, value_heads = all_heads[:rows], all_heads[rows:]
    normed = (contract_cols(key_heads, w_key) + contract_cols(value_heads, w_value)).astype(BF16)
    kv_floats = kv_input.astype(F32)
    kv_scaled = mine(kv_gain) * normed.astype(F32)
    squares = jnp.sum(kv_floats * kv_floats, axis=-1)
    dots = jnp.sum(kv_scaled * kv_floats, axis=-1)
    sums = sum_stat(jnp.stack((squares, dots)).reshape(8, -1), 4).reshape(2, rows, 1)
    kv_inverse = inverse_of(sums[0], width)
    kv_hat = kv_floats * kv_inverse
    y_slice = (
        residual_grad.astype(F32)
        + kv_inverse * (kv_scaled - kv_hat * (sums[1] * kv_inverse / width))
    ).astype(BF16)
    y_full = gather_features(y_slice, 5)
    kv_normed = (kv_hat * mine(kv_gain)).astype(BF16)
    key_weight_grad = contract_rows(kv_normed, key_heads).astype(BF16)[None]
    value_weight_grad = contract_rows(kv_normed, value_heads).astype(BF16)[None]

    ffn_floats = ffn_full.astype(F32)
    ffn_inverse = inverse_of(jnp.sum(ffn_floats * ffn_floats, axis=-1, keepdims=True), width)
    ffn_scale = ffn_floats * ffn_inverse * ffn_gain
    act_in = ffn_scale.astype(BF16)
    gate = jnp.dot(act_in, w_gate, preferred_element_type=F32)
    upper = jnp.dot(act_in, w_up, preferred_element_type=F32)
    gate_sigmoid = jax.nn.sigmoid(gate)
    gate_silu = gate * gate_sigmoid
    hidden = (gate_silu * upper).astype(BF16)
    down_grad = contract_rows(hidden, y_full).astype(BF16)[None]
    hidden_grad = contract_cols(y_full, w_down)
    gate_act = (hidden_grad * upper * gate_sigmoid * (1.0 + gate * (1.0 - gate_sigmoid))).astype(BF16)
    up_act = (hidden_grad * gate_silu).astype(BF16)
    gate_grad = contract_rows(act_in, gate_act).astype(BF16)[None]
    up_grad = contract_rows(act_in, up_act).astype(BF16)[None]
    partial_value = contract_cols(gate_act, w_gate) + contract_cols(up_act, w_up)
    row_part = jnp.sum(partial_value * ffn_scale, axis=-1).reshape(-1, HEAD)
    row_part = jnp.concatenate((row_part, jnp.zeros_like(row_part)), axis=0)
    act_slice, row_total = scatter_features(partial_value.astype(BF16), row_part, 6)
    correction = row_total[: rows // HEAD].reshape(rows, 1) / width
    hat_slice = ffn_input.astype(F32) * ffn_inverse
    input_grad = (
        y_slice.astype(F32) + ffn_inverse * (mine(ffn_gain) * act_slice - hat_slice * correction)
    ).astype(BF16)
    return (
        query_grad, input_grad, key_weight_grad, value_weight_grad, gate_grad, up_grad, down_grad,
    )


def solution(mesh):
    finer = Mesh(
        mesh.devices.reshape(4, 2, 2, mesh.shape["kvh"], mesh.shape["section"]),
        (*BLK, *FEAT),
    )
    tokens = P(BLK, FEAT)
    placed = (
        tokens, tokens, tokens, tokens, P(BLK), tokens, tokens, tokens, P(), P(),
        P(FEAT, None), P(FEAT, None), P(None, FEAT), P(None, FEAT), P(FEAT, None),
    )
    return jax.shard_map(
        on_device,
        mesh=finer,
        in_specs=placed,
        out_specs=(
            tokens,
            tokens,
            P(BLK, FEAT, None),
            P(BLK, FEAT, None),
            P(BLK, None, FEAT),
            P(BLK, None, FEAT),
            P(BLK, FEAT, None),
        ),
        check_vma=False,
    )
```

time: 670 us -> 261 us (0.39)
  waiting for transfers between devices: 473 us -> 0 us
  Pallas kernels: 0 us -> 204 us
  blocking collectives: 30.6 us -> 0 us
  local copies, waits for them, and re-layouts: 35.4 us -> 5.89 us
  other arithmetic: 38.2 us -> 13.7 us
  loops' own time: 22 us -> 0 us
  between operations: 14.1 us -> 0.85 us
  starting transfers between devices: 10.6 us -> 0 us
    all_gather x2 -> x0, waiting for transfers between devices: 299 us -> none  [the longest x1 246 us: side_by_side(): lax.all_gather(both, axis, axis=dim, tiled=True)]
    pallas_call x0 -> x7, Pallas kernels: none -> 204 us  [the longest x1 64.5 us: scatter_blocks(): pl.pallas_call(scatter16_kernel, name='scatter_blocks', out_shape=jax.Sha...]
    reduce_scatter x3 -> x0, waiting for transfers between devices: 148 us -> none  [reduced_to_own(): blocks = lax.psum_scatter(blocks, axes[k], scatter_dimension=0, tiled=True)]
    all_to_all x1 -> x0, blocking collectives: 30.6 us -> none  [sent_to_all(): return lax.all_to_all(copies, axis, split_axis=0, concat_axis=0, tiled=True)]
    all_to_all x2 -> x0, waiting for transfers between devices: 26.5 us -> none  [the longest x1 23.3 us: summed_on_arrival(): lax.all_to_all(blocks, axis, split_axis=0, concat_axis=0, tiled=True)]
    another operation x34 -> x0, loops' own time: 22 us -> none  [the longest x1 11 us: on_device(): lax.fori_loop(0, blocks, grad_block, (start_buffer, start_query))]
    reduce_sum x6 -> x1, other arithmetic: 14.4 us -> 2.73 us  [on_device(): jnp.sum(ffn_floats * ffn_floats, axis=-1, keepdims=True)]
    unnamed x59 -> x42, local copies, waits for them, and re-layouts: 12.3 us -> 1.73 us
  transfers between devices with their start and end apart: 7 -> 0, of which waited for: 7 -> 0; matrix products, arithmetic and copies ran while one was open for 5% -> 0% of each run, Pallas kernels for 0% -> 0%
where the time goes in v1:
time: 261 us; the launch traced here: 265 us
  Pallas kernels  204 us (78%)
  matrix products  40.4 us (15%)
  other arithmetic  13.7 us (5%)
  local copies, waits for them, and re-layouts  5.89 us (2%)
    pallas_call x1, Pallas kernels, scatter_blocks(): pl.pallas_call(scatter16_kernel, name='scatter_blocks', out_shape=jax.Sha...  64.5 us
    pallas_call x2, Pallas kernels, gather_features(): pl.pallas_call(gather_kernel, name=f'gather_{collective_id}', out_shape=j...  46.4 us
    pallas_call x1, Pallas kernels, gather_first(): pl.pallas_call(first_kernel, name='gather_first', out_shape=(jax.ShapeDty...  38.4 us
    pallas_call x1, Pallas kernels, scatter_features(): pl.pallas_call(scatter8_kernel, name='scatter_features', out_shape=(jax.S...  36.5 us
    dot_general x5, matrix products, contract_cols(): lax.dot_general(left, right, (((1,), (1,)), ((), ())), preferred_element_...  17.3 us
    dot_general x5, matrix products, contract_rows(): lax.dot_general(left, right, (((0,), (0,)), ((), ())), preferred_element_...  15.5 us
    pallas_call x1, Pallas kernels, attention(): pl.pallas_call(functools.partial(attention_kernel, tile=tile, scale=1.0 /...  10.2 us
    pallas_call x1, Pallas kernels, sum_stat(): pl.pallas_call(sum_stat_kernel, name=f'sum_stat_{collective_id}', out_sha...  7.77 us

profile of v1, /device:TPU:0, one launch (start us, length us, event | category | flops | bytes accessed | tf_op | source)
XLA Modules:
  0.0 264.8 jit_solution(2908745860635196757)
XLA Ops:
  0.6 0.0 copy-start
  0.6 1.4 fusion.39
  2.1 1.9 pad_add_fusion.span_ref
  4.0 1.7 pad_maximum_fusion.kv_ref
  5.7 38.4 %gather_first.1 = (bf16[2,16,512,128]{3,2,1,0:T(8,128)(2,1)}, bf16[512,3072]{1,0:T(8,128)(2,1)}) custom-call(bf16[2,512,128]{2,1,0:T(8,128)(2,1)} %pad_maximum_fusion.kv_ref, bf16[512,384]{1,0:T(8,128)(2,1)} %ffn_ref.1), custom_call_target="tpu_custom_call" | custom-call | tf_op jit(solution)/shard_map/gather_first/pallas_call | solution.py:279
  44.1 0.0 copy-start.16
  44.1 10.2 %attention.1 = (bf16[512,384]{1,0:T(8,128)(2,1)}, bf16[2,8192,128]{2,1,0:T(8,128)(2,1)}) custom-call(s32[3]{0:T(128)} %pad_add_fusion.span_ref, s32[1,512]{1,0:T(1,128)} %bitcast.49, bf16[512,384]{1,0:T(8,128)(2,1)} %q_ref.1, bf16[512,384]{1,0:T(8,128)(2,1)} %g_ref.1, bf16[2,8192,128]{2,1,0:T(8,128)(2,1)} %bitcast.43), custom_call_target="tpu_custom_call" | custom-call | tf_op jit(solution)/shard_map/attention/pallas_call | solution.py:687
  54.3 2.7 %fusion = f32[512]{0:T(512)S(1)} fusion(bf16[512,3072]{1,0:T(8,128)(2,1)} %get-tuple-element.16), kind=kLoop, calls=%fused_computation.2 | loop fusion | flops 4718080 | bytes 3147776 | tf_op jit(solution)/shard_map/reduce_sum | solution.py:744
  57.0 0.0 copy-done.16
  57.1 0.1 copy-done.1
  57.1 4.8 %fusion.35 = f32[512,512]{1,0:T(8,128)} fusion(bf16[3072,512]{1,0:T(8,128)(2,1)} %param.27, bf16[512,3072]{1,0:T(8,128)(2,1)S(1)} %copy-done.1, f32[3072]{0:T(1024)S(1)} %copy-done.16, f32[512]{0:T(512)S(1)} %add_rsqrt_fusion), kind=kOutput, calls=%fused_computation.54 | convolution fusion | flops 1616904192 | bytes 7354368 | tf_op jit(solution)/shard_map/dot_general | solution.py:747
  61.9 0.0 copy-done
  61.9 2.9 %fusion.37 = f32[512,512]{1,0:T(8,128)} fusion(bf16[3072,512]{1,0:T(8,128)(2,1)S(1)} %copy-done, bf16[512,3072]{1,0:T(8,128)(2,1)S(1)} %copy-done.1, f32[3072]{0:T(1024)S(1)} %copy-done.16, f32[512]{0:T(512)S(1)} %add_rsqrt_fusion), kind=kOutput, calls=%fused_computation.55 | convolution fusion | flops 1616904192 | bytes 7354368 | tf_op jit(solution)/shard_map/dot_general | solution.py:748
  64.8 64.5 %scatter_blocks.1 = bf16[2,512,128]{2,1,0:T(8,128)(2,1)} custom-call(bf16[2,16,512,128]{3,2,1,0:T(8,128)(2,1)} %bitcast.44), custom_call_target="tpu_custom_call" | custom-call | tf_op jit(solution)/shard_map/scatter_blocks/pallas_call | solution.py:425
  129.3 20.0 %gather_3.1 = bf16[1024,1024]{1,0:T(8,128)(2,1)} custom-call(bf16[1024,128]{1,0:T(8,128)(2,1)} %bitcast.45), custom_call_target="tpu_custom_call" | custom-call | tf_op jit(solution)/shard_map/gather_3/pallas_call | solution.py:317
  149.3 0.0 copy-start.14
  149.3 3.1 %fusion.19 = f32[512,384]{1,0:T(8,128)} fusion(bf16[384,1024]{1,0:T(8,128)(2,1)} %param.25, bf16[1024,1024]{1,0:T(8,128)(2,1)} %gather_3.1), kind=kOutput, calls=%fused_computation.35 | convolution fusion | flops 402653184 | bytes 2621440 | tf_op jit(solution)/shard_map/dot_general | solution.py:29
  152.5 0.8 dynamic_slice.7
  153.2 0.6 copy-done.19
  153.8 3.4 %fusion.26 = (f32[512]{0:T(512)S(1)}, f32[512]{0:T(512)S(1)}, f32[512,384]{1,0:T(8,128)}) fusion(bf16[512,384]{1,0:T(8,128)(2,1)} %param.20, f32[512,384]{1,0:T(8,128)} %fusion.19, bf16[384,1024]{1,0:T(8,128)(2,1)} %param.26, bf16[1024,1024]{1,0:T(8,128)(2,1)} %gather_3.1, f32[384]{0:T(512)S(1)} %dynamic_slice.7), kind=kOutput, calls=%fused_computation.42 | convolution fusion | flops 404421632 | bytes 3806720 | tf_op jit(solution)/shard_map/dot_general | solution.py:29
  157.2 0.6 pad_maximum_fusion.1
  157.8 1.3 reshape.90.x_ref
  159.1 7.8 %sum_stat_4.1 = f32[8,128]{1,0:T(8,128)} custom-call(f32[8,128]{1,0:T(8,128)} %reshape.90.x_ref), custom_call_target="tpu_custom_call" | custom-call | tf_op jit(solution)/shard_map/sum_stat_4/pallas_call | solution.py:460
  166.9 0.8 fusion.31
  167.7 0.7 rsqrt_bitcast_fusion
  168.3 0.6 copy-done.17
  168.9 0.0 copy-done.14
  168.9 2.2 fusion.24.x_ref
  171.2 26.4 %gather_5.1 = bf16[512,3072]{1,0:T(8,128)(2,1)} custom-call(bf16[512,384]{1,0:T(8,128)(2,1)} %fusion.24.x_ref), custom_call_target="tpu_custom_call" | custom-call | tf_op jit(solution)/shard_map/gather_5/pallas_call | solution.py:317
  197.6 0.0 copy-start.6
  197.6 5.6 %multiply_convert_fusion.1 = (bf16[512,512]{1,0:T(8,128)(2,1)S(1)}, bf16[512,512]{1,0:T(8,128)(2,1)S(1)}) fusion(f32[512,512]{1,0:T(8,128)} %fusion.35, f32[512,512]{1,0:T(8,128)} %fusion.37, bf16[512,3072]{1,0:T(8,128)(2,1)} %gather_5.1, bf16[512,3072]{1,0:T(8,128)(2,1)} %param.29), kind=kOutput, calls=%fused_computation.26 | convolution fusion | flops 1614020608 | bytes 9437184 | tf_op jit(solution)/shard_map/dot_general | solution.py:29
  203.2 0.0 copy-start.12
  203.3 0.0 copy-start.10
  203.3 0.0 copy-done.6
  203.3 0.0 copy-start.2
  203.3 1.8 fusion.40
  205.1 0.0 copy-done.12
  205.1 0.0 copy-done.10
  205.1 0.4 copy-done.2
  205.5 3.4 %fusion.4 = (f32[512]{0:T(512)S(1)}, bf16[512,3072]{1,0:T(8,128)(2,1)}) fusion(bf16[512,3072]{1,0:T(8,128)(2,1)S(1)} %copy-done.2, f32[3072]{0:T(1024)S(1)} %copy-done.16, f32[512]{0:T(512)S(1)} %add_rsqrt_fusion, f32[512,3072]{1,0:T(8,128)S(1)} %fusion.40, bf16[512,512]{1,0:T(8,128)(2,1)S(1)} %get-tuple-element.23, bf16[3072,512]{1,0:T(8,128)(2,1)S(1)} %copy-done), kind=kOutput, calls=%fused_computation.6 | convolution fusion | flops 1621622272 | bytes 16269312 | tf_op jit(solution)/shard_map/dot_general | solution.py:29
  208.9 0.6 concatenate.3.stat_ref
  209.5 36.5 %scatter_features.1 = (f32[512,384]{1,0:T(8,128)}, f32[8,128]{1,0:T(8,128)}) custom-call(bf16[512,3072]{1,0:T(8,128)(2,1)} %get-tuple-element.22.part_ref, f32[8,128]{1,0:T(8,128)} %concatenate.3.stat_ref), custom_call_target="tpu_custom_call" | custom-call | tf_op jit(solution)/shard_map/scatter_features/pallas_call | solution.py:555
  246.0 0.0 copy-start.7
  246.0 0.0 copy-start.15
  246.0 0.0 copy-start.18
  246.0 0.0 copy-start.20
  246.0 0.8 multiply_bitcast_fusion
  246.9 0.1 dynamic_slice.8
  247.0 0.0 copy-done.5
  247.0 2.3 add_convert_fusion
  249.3 3.1 %fusion.8 = bf16[1,384,1024]{2,1,0:T(8,128)(2,1)} fusion(bf16[1024,1024]{1,0:T(8,128)(2,1)} %gather_3.1, bf16[512,384]{1,0:T(8,128)(2,1)} %param.20, f32[512]{0:T(512)} %copy-done.17, f32[384]{0:T(512)} %copy-done.19), kind=kOutput, calls=%fused_computation.16 | convolution fusion | flops 403832832 | bytes 2232320 | tf_op jit(solution)/shard_map/dot_general | solution.py:25
  252.3 0.0 copy-done.7
  252.3 0.0 copy-done.15
  252.3 0.0 copy-done.18
  252.3 0.0 copy-done.20
  252.3 1.6 fusion.9
  253.9 0.0 copy-done.3
  253.9 0.0 copy-done.13
  253.9 3.6 %fusion.5 = bf16[1,3072,512]{2,1,0:T(8,128)(2,1)} fusion(bf16[512,512]{1,0:T(8,128)(2,1)S(1)} %copy-done.13, bf16[512,3072]{1,0:T(8,128)(2,1)S(1)} %copy-done.3, f32[3072]{0:T(1024)S(1)} %copy-done.16, f32[512]{0:T(512)S(1)} %add_rsqrt_fusion), kind=kOutput, calls=%fused_computation.11 | convolution fusion | flops 1618477056 | bytes 6830080 | tf_op jit(solution)/shard_map/dot_general | solution.py:25
  257.6 0.0 copy-done.11
  257.6 3.6 %fusion.6 = bf16[1,3072,512]{2,1,0:T(8,128)(2,1)} fusion(bf16[512,512]{1,0:T(8,128)(2,1)S(1)} %copy-done.11, bf16[512,3072]{1,0:T(8,128)(2,1)S(1)} %copy-done.3, f32[3072]{0:T(1024)S(1)} %copy-done.16, f32[512]{0:T(512)S(1)} %add_rsqrt_fusion), kind=kOutput, calls=%fused_computation.12 | convolution fusion | flops 1618477056 | bytes 6830080 | tf_op jit(solution)/shard_map/dot_general | solution.py:25
  261.2 0.0 copy-done.4
  261.2 0.0 copy-done.8
  261.2 3.6 %fusion.7 = bf16[1,512,3072]{2,1,0:T(8,128)(2,1)} fusion(bf16[512,3072]{1,0:T(8,128)(2,1)S(1)} %copy-done.4, f32[512,512]{1,0:T(8,128)S(1)} %copy-done.9, f32[512,512]{1,0:T(8,128)S(1)} %copy-done.8), kind=kOutput, calls=%fused_computation.13 | convolution fusion | flops 1613758464 | bytes 8388608 | tf_op jit(solution)/shard_map/dot_general | solution.py:25
  (12 shorter events, 0.0 us)
Async XLA Ops:
  0.6 61.3 %copy-start = (bf16[3072,512]{1,0:T(8,128)(2,1)S(1)}, bf16[3072,512]{1,0:T(8,128)(2,1)}, u32[]{:S(2)}) copy-start(bf16[3072,512]{1,0:T(8,128)(2,1)} %param.28) | copy-start | bytes 9437188
  44.1 13.0 %copy-start.16 = (f32[3072]{0:T(1024)S(1)}, f32[3072]{0:T(1024)}, u32[]{:S(2)}) copy-start(f32[3072]{0:T(1024)} %param.24) | copy-start | bytes 36868
  54.3 2.8 %copy-start.1 = (bf16[512,3072]{1,0:T(8,128)(2,1)S(1)}, bf16[512,3072]{1,0:T(8,128)(2,1)}, u32[]{:S(2)}) copy-start(bf16[512,3072]{1,0:T(8,128)(2,1)} %get-tuple-element.16) | copy-start | bytes 9437188
  149.3 19.6 %copy-start.14 = (bf16[512,384]{1,0:T(8,128)(2,1)S(1)}, bf16[512,384]{1,0:T(8,128)(2,1)}, u32[]{:S(2)}) copy-start(bf16[512,384]{1,0:T(8,128)(2,1)} %param.21) | copy-start | bytes 1179652
  153.2 0.6 copy-start.19
  168.3 0.6 copy-start.17
  197.6 5.7 %copy-start.6 = (bf16[3072,512]{1,0:T(8,128)(2,1)S(1)}, bf16[3072,512]{1,0:T(8,128)(2,1)}, u32[]{:S(2)}) copy-start(bf16[3072,512]{1,0:T(8,128)(2,1)} %param.27) | copy-start | bytes 9437188
  203.2 1.9 copy-start.12
  203.3 1.9 copy-start.10
  203.3 2.3 copy-start.2
  208.9 38.1 %copy-start.5 = (bf16[512,384]{1,0:T(8,128)(2,1)S(1)}, bf16[512,384]{1,0:T(8,128)(2,1)}, u32[]{:S(2)}) copy-start(bf16[512,384]{1,0:T(8,128)(2,1)} %fusion.24.x_ref) | copy-start | bytes 1179652
  246.0 6.3 %copy-start.7 = (bf16[1024,1024]{1,0:T(8,128)(2,1)S(1)}, bf16[1024,1024]{1,0:T(8,128)(2,1)}, u32[]{:S(2)}) copy-start(bf16[1024,1024]{1,0:T(8,128)(2,1)} %gather_3.1) | copy-start | bytes 6291460
  246.0 6.3 %copy-start.15 = (bf16[512,384]{1,0:T(8,128)(2,1)S(1)}, bf16[512,384]{1,0:T(8,128)(2,1)}, u32[]{:S(2)}) copy-start(bf16[512,384]{1,0:T(8,128)(2,1)} %param.20) | copy-start | bytes 1179652
  246.0 6.3 %copy-start.18 = (f32[512]{0:T(512)S(1)}, f32[512]{0:T(512)}, u32[]{:S(2)}) copy-start(f32[512]{0:T(512)} %copy-done.17) | copy-start | bytes 6148
  246.0 6.3 %copy-start.20 = (f32[384]{0:T(512)S(1)}, f32[384]{0:T(512)}, u32[]{:S(2)}) copy-start(f32[384]{0:T(512)} %copy-done.19) | copy-start | bytes 4612
  249.2 4.7 %copy-start.3 = (bf16[512,3072]{1,0:T(8,128)(2,1)S(1)}, bf16[512,3072]{1,0:T(8,128)(2,1)}, u32[]{:S(2)}) copy-start(bf16[512,3072]{1,0:T(8,128)(2,1)} %get-tuple-element.16) | copy-start | bytes 9437188
  249.3 4.7 %copy-start.13 = (bf16[512,512]{1,0:T(8,128)(2,1)S(1)}, bf16[512,512]{1,0:T(8,128)(2,1)}, u32[]{:S(2)}) copy-start(bf16[512,512]{1,0:T(8,128)(2,1)} %copy-done.12) | copy-start | bytes 1572868
  253.9 3.6 %copy-start.11 = (bf16[512,512]{1,0:T(8,128)(2,1)S(1)}, bf16[512,512]{1,0:T(8,128)(2,1)}, u32[]{:S(2)}) copy-start(bf16[512,512]{1,0:T(8,128)(2,1)} %copy-done.10) | copy-start | bytes 1572868
  257.6 3.6 %copy-start.4 = (bf16[512,3072]{1,0:T(8,128)(2,1)S(1)}, bf16[512,3072]{1,0:T(8,128)(2,1)}, u32[]{:S(2)}) copy-start(bf16[512,3072]{1,0:T(8,128)(2,1)} %gather_5.1) | copy-start | bytes 9437188
  257.6 3.6 %copy-start.8 = (f32[512,512]{1,0:T(8,128)S(1)}, f32[512,512]{1,0:T(8,128)}, u32[]{:S(2)}) copy-start(f32[512,512]{1,0:T(8,128)} %fusion.35) | copy-start | bytes 3145732
  257.6 3.6 %copy-start.9 = (f32[512,512]{1,0:T(8,128)S(1)}, f32[512,512]{1,0:T(8,128)}, u32[]{:S(2)}) copy-start(f32[512,512]{1,0:T(8,128)} %fusion.37) | copy-start | bytes 3145732
